TPU v7x, 32 devices: a whole 2x2x4 slice. The times are simulated.
32 devices in a mesh: groups: 2 (over y), blk: 4 (over z), split: 2 (over x), sub: 2 (over core).
Axes of the slice: x: 2, y: 2, z: 4, core: 2. Of those that a mesh axis runs over, the one named last changes fastest.
Arguments:
- attention_output_rows: bfloat16 [1024, 8192], P(('groups', 'blk'), 'split'), parts along dimension 0, may hold values from -6 to 6
- residual: bfloat16 [1024, 8192], P(('groups', 'split'), ('blk', 'sub')), parts along dimension 0, may hold values from -6 to 6
- output_projection_weight: bfloat16 [8192, 8192], P('split', ('blk', 'sub')), may hold values from -0.0625 to 0.0625
- down_adapter_bank: bfloat16 [4, 64, 8192], P('blk', None, 'split'), may hold values from -0.0625 to 0.0625
- up_adapter_bank: bfloat16 [4, 64, 8192], P('split', None, ('blk', 'sub')), may hold values from -0.75 to 0.75
- rollout_row_tenant: int32 [1024], P('groups'), parts along dimension 0, may hold values from 0 to 3, as said below
- tenant_bank_entry: int32 [4], replicated, may hold values from 0 to 3, each once
- tenant_live_rank: int32 [4], replicated, may hold values from 16 to 64, as said below
Outputs:
- layer_out: bfloat16 [1024, 8192], P(('groups', 'split'), ('blk', 'sub')), parts along dimension 0
There are 2 independent parts, one for each index of `groups`. A program takes and returns all parts, laid end to end along the dimension named above; an argument that names none is the same for every part. Nothing has to cross between parts.
Inputs may be any that keep to these rules, and one draw needn't show every extreme that they name: `rollout_row_tenant`: every tenant owns at least one row of every part. `tenant_live_rank`: some tenant has the full rank 64.
All inputs are finite; a program needn't handle non-finite values.
Results may differ from a plain program's by a relative error of at most 0.0038.
Values may be sent and summed in bfloat16 or wider, within the bound.
A program may use at most 64 MiB of HBM per device.

v0:
```python
import jax
import jax.numpy as jnp
from jax import lax
from jax.sharding import PartitionSpec as P


def shards(
    attention_output_rows,
    residual,
    output_projection_weight,
    down_adapter_bank,
    up_adapter_bank,
    rollout_row_tenant,
    tenant_bank_entry,
    tenant_live_rank,
):
    out_cols = output_projection_weight.shape[1]
    feat_width = attention_output_rows.shape[1]
    rank_mask_rows = down_adapter_bank.shape[1]
    gathered_down_maps = lax.all_gather(down_adapter_bank, "blk", axis=0, tiled=True)
    tenant_count = gathered_down_maps.shape[0]
    total_rows = rollout_row_tenant.shape[0]
    tenant_ids = jnp.arange(tenant_count, dtype=jnp.int32)
    tenant_hot = (rollout_row_tenant[:, None] == tenant_ids[None, :]).astype(jnp.int32)
    slot_all = jnp.sum(tenant_hot * tenant_bank_entry[None, :], axis=1)
    rank_all = jnp.sum(tenant_hot * tenant_live_rank[None, :], axis=1)
    down_cols = gathered_down_maps.reshape(tenant_count * rank_mask_rows, feat_width).T
    joined = jnp.concatenate([output_projection_weight, down_cols], axis=1)
    own_count = total_rows // lax.axis_size("split")
    own_start = lax.axis_index("split") * own_count
    own_slot = lax.dynamic_slice_in_dim(slot_all, own_start, own_count, 0)
    own_rank = lax.dynamic_slice_in_dim(rank_all, own_start, own_count, 0)
    own_hot = own_slot[:, None] == tenant_ids[None, :]
    full = jnp.dot(
        lax.all_gather(attention_output_rows, "blk", axis=0, tiled=True),
        joined,
        preferred_element_type=jnp.float32,
    )
    piece_hot = slot_all[:, None] == tenant_ids[None, :]
    values = full[:, out_cols:]
    shaped = values.reshape(values.shape[0], tenant_count, rank_mask_rows)
    products = jnp.concatenate(
        [
            full[:, :out_cols],
            jnp.sum(jnp.where(piece_hot[:, :, None], shaped, jnp.zeros((), jnp.float32)), axis=1),
        ],
        axis=1,
    )
    summed = lax.psum_scatter(products, "split", scatter_dimension=0, tiled=True)
    frozen_output_term = summed[:, :out_cols]
    low_rank = summed[:, out_cols:]
    gathered_up_maps = lax.all_gather(up_adapter_bank, "split", axis=0, tiled=True)
    kept_mask = jnp.arange(rank_mask_rows, dtype=jnp.int32)[None, :] < own_rank[:, None]
    scaling = rank_mask_rows / own_rank.astype(jnp.float32)
    low_scaled = jnp.where(
        kept_mask, low_rank * scaling[:, None], jnp.zeros((), jnp.float32)
    ).astype(jnp.bfloat16)
    rank_expanded_rows = jnp.where(
        own_hot[:, :, None], low_scaled[:, None, :], jnp.zeros((), jnp.bfloat16)
    ).reshape(own_count, tenant_count * rank_mask_rows)
    adapter_output_term = jnp.dot(
        rank_expanded_rows,
        gathered_up_maps.reshape(tenant_count * rank_mask_rows, out_cols),
        preferred_element_type=jnp.float32,
    )
    return (residual.astype(jnp.float32) + frozen_output_term + adapter_output_term).astype(
        jnp.bfloat16
    )


def solution(mesh):
    in_specs = (
        P(("groups", "blk"), "split"),
        P(("groups", "split"), ("blk", "sub")),
        P("split", ("blk", "sub")),
        P("blk", None, "split"),
        P("split", None, ("blk", "sub")),
        P("groups"),
        P(),
        P(),
    )
    out_specs = P(("groups", "split"), ("blk", "sub"))
    return jax.shard_map(shards, mesh=mesh, in_specs=in_specs, out_specs=out_specs, check_vma=False)
```

profile of v0, /device:TPU:0, one launch (start us, length us, event | category | flops | bytes accessed | tf_op | source)
XLA Modules:
  0.0 194.9 jit_solution(4081771632402627207)
XLA Ops:
  6.5 0.0 all-gather.3.cloned.1.call-start
  6.5 0.7 all-gather.3.cloned.1.call-update
  7.3 0.0 all-gather.5.cloned.1.call-start
  7.3 0.7 all-gather.5.cloned.1.call-update
  8.0 0.0 reduce-scatter.2.cloned.1.call-start
  8.1 0.8 select_reduce_fusion.1
  8.8 48.5 %all-gather.3.cloned.1.call-done = bf16[4,64,4096]{2,1,0:T(8,128)(2,1)} async-done(((bf16[1,64,4096]{2,1,0:T(8,128)(2,1)}), bf16[4,64,4096]{2,1,0:T(8,128)(2,1)}) %all-gather.3.cloned.1.call-update) | async-done | bytes 2097168 | tf_op jit(solution)/shard_map/all_gather | solution.py:20
  57.3 3.3 %copy.18 = bf16[256,4096]{0,1:T(8,128)(2,1)S(1)} copy(bf16[256,4096]{1,0:T(8,128)(2,1)} %bitcast.14) | data formatting | bytes 4194304 | tf_op jit(solution)/shard_map/reshape | solution.py:27
  60.6 77.9 %all-gather.5.cloned.1.call-done = bf16[512,4096]{1,0:T(8,128)(2,1)} async-done(((bf16[128,4096]{1,0:T(8,128)(2,1)}), bf16[512,4096]{1,0:T(8,128)(2,1)}) %all-gather.5.cloned.1.call-update) | async-done | bytes 4194320 | tf_op jit(solution)/shard_map/all_gather | solution.py:35
  138.5 9.7 %fusion.4 = f32[512,1280]{0,1:T(8,128)S(1)} fusion(bf16[512,4096]{1,0:T(8,128)(2,1)} %all-gather.5.cloned.1.call-done, bf16[4096,256]{1,0:T(8,128)(2,1)S(1)} %bitcast.15, bf16[4096,1024]{1,0:T(8,128)(2,1)} %param.10), kind=kOutput, calls=%fused_computation.4 | convolution fusion | flops 5389680640 | bytes 17301504 | tf_op jit(solution)/shard_map/dot_general | solution.py:34
  148.2 0.2 slice.16
  148.4 0.1 select_reduce_fusion
  148.5 0.0 copy-start
  148.5 1.6 pad_maximum_fusion
  150.0 0.0 copy-start.1
  150.0 0.0 reduce-scatter.2.cloned.1.call-update
  150.1 0.1 dynamic_slice.6
  150.1 0.0 copy-done
  150.1 0.2 copy.17
  150.4 0.1 convert_divide_fusion
  150.4 0.5 copy-done.1
  151.0 12.9 %all_gather.11 = bf16[4,64,1024]{2,1,0:T(8,128)(2,1)S(1)} all-gather(bf16[2,64,1024]{2,1,0:T(8,128)(2,1)S(1)} %copy-done.1), channel_id=1, replica_groups=mesh['groups'=2,'blk'=4,'split'=2,'sub'=2] {'split'}, dimensions={0}, use_global_device_ids=true | all-gather | bytes 786432 | tf_op jit(solution)/shard_map/all_gather | solution.py:52
  163.9 21.1 %reduce-scatter.2.cloned.1.call-done = f32[256,1088]{0,1:T(8,128)} async-done(((f32[512,1088]{0,1:T(8,128)}), f32[256,1088]{0,1:T(8,128)}) %reduce-scatter.2.cloned.1.call-update) | async-done | bytes 1114128 | tf_op jit(solution)/shard_map/reduce_scatter | solution.py:49
  185.0 0.9 fusion.12
  185.8 1.6 fusion.8
  187.4 1.0 copy.20
  (3 shorter events, 0.1 us)
Async XLA Ops:
  6.5 50.8 %all-gather.3.cloned.1.call-start = ((), (), s32[]{:S(2)}) async-start(), calls=%async_computation.1 | async-start | bytes 2621440 | tf_op jit(solution)/shard_map/all_gather | solution.py:20
  7.3 131.2 %all-gather.5.cloned.1.call-start = ((), (), s32[]{:S(2)}) async-start(), calls=%async_computation.2 | async-start | bytes 5242880 | tf_op jit(solution)/shard_map/all_gather | solution.py:35
  8.0 177.0 %reduce-scatter.2.cloned.1.call-start = ((), (), s32[]{:S(2)}) async-start(), calls=%async_computation.3 | async-start | bytes 3342336 | tf_op jit(solution)/shard_map/reduce_scatter | solution.py:49
  148.5 1.7 copy-start
  150.0 0.9 copy-start.1
Sparse Core Ops, SparseCore 0:
  8.9 48.3 all-gather.2
  58.9 79.5 all-gather.4
  150.2 34.7 reduce-scatter.1
where the time goes:
time: 195 us
  waiting for transfers between devices  149 us (76%)
  between operations  13.2 us (7%)
  blocking collectives  12.9 us (7%)
  matrix products  11.3 us (6%)
  local copies, waits for them, and re-layouts  5.31 us (3%)
  other arithmetic  3.35 us (2%)
    all_gather x1, waiting for transfers between devices, shards(): lax.all_gather(attention_output_rows, 'blk', axis=0, tiled=True)  77.9 us
    all_gather x1, waiting for transfers between devices, shards(): lax.all_gather(down_adapter_bank, 'blk', axis=0, tiled=True)  48.5 us
    reduce_scatter x1, waiting for transfers between devices, shards(): lax.psum_scatter(products, 'split', scatter_dimension=0, tiled=True)  21.1 us
    all_gather x1, blocking collectives, shards(): lax.all_gather(up_adapter_bank, 'split', axis=0, tiled=True)  12.9 us
    dot_general x1, matrix products, shards(): jnp.dot(lax.all_gather(attention_output_rows, 'blk', axis=0, tiled=True),...  9.71 us
  transfers between devices with their start and end apart: 3, of which 3 were waited for; matrix products, arithmetic and copies ran while one was open for 2% of the time, Pallas kernels for 0%

commit v1 on v0

--- a/solution.py
+++ b/solution.py
@@ -2,6 +2,12 @@
 import jax.numpy as jnp
 from jax import lax
 from jax.sharding import PartitionSpec as P
+
+
+def laid_out(parts, dim):
+    dims = list(parts.shape[1:])
+    dims[dim] *= parts.shape[0]
+    return jnp.moveaxis(parts, 0, dim).reshape(dims)
 
 
 def shards(
@@ -17,7 +23,19 @@
     out_cols = output_projection_weight.shape[1]
     feat_width = attention_output_rows.shape[1]
     rank_mask_rows = down_adapter_bank.shape[1]
-    gathered_down_maps = lax.all_gather(down_adapter_bank, "blk", axis=0, tiled=True)
+    size = lax.axis_size("blk")
+    pairs = [(i, (i + 1) % size) for i in range(size)]
+    back = [(b, a) for a, b in pairs]
+    lower, upper = ([], [])
+    for step in range(size - 1):
+        if step % 2 == 0:
+            lower.append(lax.ppermute(lower[-1] if lower else down_adapter_bank, "blk", pairs))
+        else:
+            upper.append(lax.ppermute(upper[-1] if upper else down_adapter_bank, "blk", back))
+    blocks = jnp.stack([*lower[::-1], down_adapter_bank, *upper])
+    shift = lax.axis_index("blk") - len(lower)
+    blocks = blocks[(jnp.arange(size) - shift) % size]
+    gathered_down_maps = laid_out(blocks, 0)
     tenant_count = gathered_down_maps.shape[0]
     total_rows = rollout_row_tenant.shape[0]
     tenant_ids = jnp.arange(tenant_count, dtype=jnp.int32)

time: 195 us -> 173 us (0.89)
  waiting for transfers between devices: 149 us -> 111 us
  starting transfers between devices: 0.08 us -> 11.8 us
  local copies, waits for them, and re-layouts: 5.31 us -> 7.7 us
    ppermute x0 -> x3, waiting for transfers between devices: none -> 50.6 us  [the longest x1 32.7 us: shards(): lax.ppermute(upper[-1] if upper else down_adapter_bank, 'blk', back)]
    all_gather x1 -> x0, waiting for transfers between devices: 48.5 us -> none  [shards(): lax.all_gather(down_adapter_bank, 'blk', axis=0, tiled=True)]
    all_gather x1, waiting for transfers between devices: 77.9 us -> 38 us  [shards(): lax.all_gather(attention_output_rows, 'blk', axis=0, tiled=True)]
    ppermute x0 -> x3, starting transfers between devices: none -> 11.8 us  [the longest x2 9.67 us: shards(): lax.ppermute(lower[-1] if lower else down_adapter_bank, 'blk', pairs)]
    another operation x0 -> x1, local copies, waits for them, and re-layouts: none -> 3.27 us  [shards(): gathered_down_maps.reshape(tenant_count * rank_mask_rows, feat_width)]
    reshape x1 -> x0, local copies, waits for them, and re-layouts: 3.27 us -> none  [shards(): gathered_down_maps.reshape(tenant_count * rank_mask_rows, feat_width)]
    gather x0 -> x1, local copies, waits for them, and re-layouts: none -> 2 us  [shards(): blocks = blocks[(jnp.arange(size) - shift) % size]]
  transfers between devices with their start and end apart: 3 -> 5, of which waited for: 3 -> 5; matrix products, arithmetic and copies ran while one was open for 2% -> 4% of each run, Pallas kernels for 0% -> 0%
where the time goes in v1:
time: 173 us
  waiting for transfers between devices  111 us (64%)
  between operations  13.5 us (8%)
  blocking collectives  12.9 us (7%)
  starting transfers between devices  11.8 us (7%)
  matrix products  11.3 us (7%)
  local copies, waits for them, and re-layouts  7.7 us (4%)
  other arithmetic  4.69 us (3%)
    all_gather x1, waiting for transfers between devices, shards(): lax.all_gather(attention_output_rows, 'blk', axis=0, tiled=True)  38 us
    ppermute x1, waiting for transfers between devices, shards(): lax.ppermute(upper[-1] if upper else down_adapter_bank, 'blk', back)  32.7 us
    reduce_scatter x1, waiting for transfers between devices, shards(): lax.psum_scatter(products, 'split', scatter_dimension=0, tiled=True)  21.4 us
    ppermute x2, waiting for transfers between devices, shards(): lax.ppermute(lower[-1] if lower else down_adapter_bank, 'blk', pairs)  17.9 us
    all_gather x1, blocking collectives, shards(): lax.all_gather(up_adapter_bank, 'split', axis=0, tiled=True)  12.9 us
    dot_general x1, matrix products, shards(): jnp.dot(lax.all_gather(attention_output_rows, 'blk', axis=0, tiled=True),...  9.71 us
    ppermute x2, starting transfers between devices, shards(): lax.ppermute(lower[-1] if lower else down_adapter_bank, 'blk', pairs)  9.67 us
  transfers between devices with their start and end apart: 5, of which 5 were waited for; matrix products, arithmetic and copies ran while one was open for 4% of the time, Pallas kernels for 0%

profile of v1, /device:TPU:0, one launch (start us, length us, event | category | flops | bytes accessed | tf_op | source)
XLA Modules:
  0.0 172.6 jit_solution(15908623694549073033)
XLA Ops:
  6.5 0.0 all-gather.2.cloned.1.call-start
  6.5 0.7 all-gather.2.cloned.1.call-update
  7.3 0.0 reduce-scatter.2.cloned.1.call-start
  7.3 3.1 %collective-permute-start = (bf16[1,64,4096]{2,1,0:T(8,128)(2,1)}, bf16[1,64,4096]{2,1,0:T(8,128)(2,1)S(1)}, u32[]{:S(2)}, u32[]{:S(2)}) collective-permute-start(bf16[1,64,4096]{2,1,0:T(8,128)(2,1)} %param.11), channel_id=1, source_target_pairs={{0,4},{4,8},{8,12},{12,0},{1,5},{5,9},{9,13},{13,1},{2,6},{6,10},{... | collective-permute-start | bytes 1572872 | tf_op jit(solution)/shard_map/ppermute | solution.py:32
  10.4 2.1 %collective-permute-start.2 = (bf16[1,64,4096]{2,1,0:T(8,128)(2,1)}, bf16[1,64,4096]{2,1,0:T(8,128)(2,1)S(1)}, u32[]{:S(2)}, u32[]{:S(2)}) collective-permute-start(bf16[1,64,4096]{2,1,0:T(8,128)(2,1)} %param.11), channel_id=1, source_target_pairs={{4,0},{8,4},{12,8},{0,12},{5,1},{9,5},{13,9},{1,13},{6,2},{10,6},{... | collective-permute-start | bytes 1572872 | tf_op jit(solution)/shard_map/ppermute | solution.py:34
  12.5 13.9 %collective-permute-done = bf16[1,64,4096]{2,1,0:T(8,128)(2,1)S(1)} collective-permute-done((bf16[1,64,4096]{2,1,0:T(8,128)(2,1)}, bf16[1,64,4096]{2,1,0:T(8,128)(2,1)S(1)}, u32[]{:S(2)}, u32[]{:S(2)}) %collective-permute-start) | collective-permute-done | bytes 524320 | tf_op jit(solution)/shard_map/ppermute | solution.py:32
  26.4 6.6 %collective-permute-start.1 = (bf16[1,64,4096]{2,1,0:T(8,128)(2,1)S(1)}, bf16[1,64,4096]{2,1,0:T(8,128)(2,1)S(1)}, u32[]{:S(2)}, u32[]{:S(2)}) collective-permute-start(bf16[1,64,4096]{2,1,0:T(8,128)(2,1)S(1)} %collective-permute-done), channel_id=1, source_target_pairs={{0,4},{4,8},{8,12},{12,0},{1,5},{5,9},{9,13},{13,1},{2,6},{6,10},{... | collective-permute-start | bytes 1572872 | tf_op jit(solution)/shard_map/ppermute | solution.py:32
  33.0 0.8 select_reduce_fusion.1
  33.8 32.7 %collective-permute-done.2 = bf16[1,64,4096]{2,1,0:T(8,128)(2,1)S(1)} collective-permute-done((bf16[1,64,4096]{2,1,0:T(8,128)(2,1)}, bf16[1,64,4096]{2,1,0:T(8,128)(2,1)S(1)}, u32[]{:S(2)}, u32[]{:S(2)}) %collective-permute-start.2) | collective-permute-done | bytes 524320 | tf_op jit(solution)/shard_map/ppermute | solution.py:34
  66.5 4.0 %collective-permute-done.1 = bf16[1,64,4096]{2,1,0:T(8,128)(2,1)S(1)} collective-permute-done((bf16[1,64,4096]{2,1,0:T(8,128)(2,1)S(1)}, bf16[1,64,4096]{2,1,0:T(8,128)(2,1)S(1)}, u32[]{:S(2)}, u32[]{:S(2)}) %collective-permute-start.1) | collective-permute-done | bytes 524320 | tf_op jit(solution)/shard_map/ppermute | solution.py:32
  70.5 1.3 maximum_bitcast_fusion
  71.8 2.0 %gather_fusion = bf16[4,64,4096]{2,1,0:T(8,128)(2,1)} fusion(bf16[4,64,4096]{2,1,0:T(8,128)(2,1)S(1)} %maximum_bitcast_fusion, s32[1024]{0:T(1024)S(1)} %pad_clamp_fusion), kind=kCustom, calls=%fused_computation | custom fusion | bytes 4194320 | tf_op jit(solution)/shard_map/gather | solution.py:37
  73.8 3.3 %copy.18 = bf16[256,4096]{0,1:T(8,128)(2,1)S(1)} copy(bf16[256,4096]{1,0:T(8,128)(2,1)} %bitcast.21) | data formatting | bytes 4194304 | tf_op jit(solution)/shard_map/reshape;reshape | solution.py:45
  77.1 38.0 %all-gather.2.cloned.1.call-done = bf16[512,4096]{1,0:T(8,128)(2,1)} async-done(((bf16[128,4096]{1,0:T(8,128)(2,1)}), bf16[512,4096]{1,0:T(8,128)(2,1)}) %all-gather.2.cloned.1.call-update) | async-done | bytes 4194320 | tf_op jit(solution)/shard_map/all_gather | solution.py:53
  115.1 9.7 %fusion.4 = f32[512,1280]{0,1:T(8,128)S(1)} fusion(bf16[512,4096]{1,0:T(8,128)(2,1)} %all-gather.2.cloned.1.call-done, bf16[4096,256]{1,0:T(8,128)(2,1)S(1)} %bitcast.23, bf16[4096,1024]{1,0:T(8,128)(2,1)} %param.10), kind=kOutput, calls=%fused_computation.5 | convolution fusion | flops 5389680640 | bytes 17301504 | tf_op jit(solution)/shard_map/dot_general | solution.py:52
  124.9 0.2 slice.18
  125.0 0.1 select_reduce_fusion
  125.1 1.6 pad_maximum_fusion
  126.7 0.0 copy-start
  126.7 0.0 copy-start.1
  126.7 0.0 reduce-scatter.2.cloned.1.call-update
  126.7 0.1 dynamic_slice.6
  126.8 0.9 copy-done
  127.7 0.2 copy.17
  127.9 0.1 convert_divide_fusion
  128.0 0.0 copy-done.1
  128.0 12.9 %all_gather.7 = bf16[4,64,1024]{2,1,0:T(8,128)(2,1)S(1)} all-gather(bf16[2,64,1024]{2,1,0:T(8,128)(2,1)S(1)} %copy-done.1), channel_id=1, replica_groups=mesh['groups'=2,'blk'=4,'split'=2,'sub'=2] {'split'}, dimensions={0}, use_global_device_ids=true | all-gather | bytes 786432 | tf_op jit(solution)/shard_map/all_gather | solution.py:70
  140.9 21.4 %reduce-scatter.2.cloned.1.call-done = f32[256,1088]{0,1:T(8,128)} async-done(((f32[512,1088]{0,1:T(8,128)}), f32[256,1088]{0,1:T(8,128)}) %reduce-scatter.2.cloned.1.call-update) | async-done | bytes 1114128 | tf_op jit(solution)/shard_map/reduce_scatter | solution.py:67
  162.3 0.9 fusion.12
  163.2 1.6 fusion.8
  164.8 1.0 copy.20
  (5 shorter events, 0.1 us)
Async XLA Ops:
  6.5 108.6 %all-gather.2.cloned.1.call-start = ((), (), s32[]{:S(2)}) async-start(), calls=%async_computation.1 | async-start | bytes 5242880 | tf_op jit(solution)/shard_map/all_gather | solution.py:53
  7.3 155.1 %reduce-scatter.2.cloned.1.call-start = ((), (), s32[]{:S(2)}) async-start(), calls=%async_computation.2 | async-start | bytes 3342336 | tf_op jit(solution)/shard_map/reduce_scatter | solution.py:67
  7.3 19.1 %collective-permute-start = (bf16[1,64,4096]{2,1,0:T(8,128)(2,1)}, bf16[1,64,4096]{2,1,0:T(8,128)(2,1)S(1)}, u32[]{:S(2)}, u32[]{:S(2)}) collective-permute-start(bf16[1,64,4096]{2,1,0:T(8,128)(2,1)} %param.11), channel_id=1, source_target_pairs={{0,4},{4,8},{8,12},{12,0},{1,5},{5,9},{9,13},{13,1},{2,6},{6,10},{... | collective-permute-start | bytes 1572872 | tf_op jit(solution)/shard_map/ppermute | solution.py:32
  10.4 56.1 %collective-permute-start.2 = (bf16[1,64,4096]{2,1,0:T(8,128)(2,1)}, bf16[1,64,4096]{2,1,0:T(8,128)(2,1)S(1)}, u32[]{:S(2)}, u32[]{:S(2)}) collective-permute-start(bf16[1,64,4096]{2,1,0:T(8,128)(2,1)} %param.11), channel_id=1, source_target_pairs={{4,0},{8,4},{12,8},{0,12},{5,1},{9,5},{13,9},{1,13},{6,2},{10,6},{... | collective-permute-start | bytes 1572872 | tf_op jit(solution)/shard_map/ppermute | solution.py:34
  26.4 44.1 %collective-permute-start.1 = (bf16[1,64,4096]{2,1,0:T(8,128)(2,1)S(1)}, bf16[1,64,4096]{2,1,0:T(8,128)(2,1)S(1)}, u32[]{:S(2)}, u32[]{:S(2)}) collective-permute-start(bf16[1,64,4096]{2,1,0:T(8,128)(2,1)S(1)} %collective-permute-done), channel_id=1, source_target_pairs={{0,4},{4,8},{8,12},{12,0},{1,5},{5,9},{9,13},{13,1},{2,6},{6,10},{... | collective-permute-start | bytes 1572872 | tf_op jit(solution)/shard_map/ppermute | solution.py:32
  126.7 1.0 copy-start
  126.7 1.3 copy-start.1
Sparse Core Ops, SparseCore 0:
  8.9 106.1 all-gather.1
  126.8 35.4 reduce-scatter.1
